TPU v7x, 256 devices: a whole 4x4x8 slice. The times are simulated.
256 devices in a mesh: section: 4 (over x), tok: 64 (over y, z, core).
Axes of the slice: x: 4, y: 4, z: 8, core: 2. Of those that a mesh axis runs over, the one named last changes fastest.
Arguments:
- tracks: bfloat16 [4, 64, 128, 512], P('section', 'tok'), may hold values from -6 to 6
- valid_steps: int32 [4, 64, 128], P(None, 'tok'), may hold values from 0 to 1, as said below
- hilbert_order: int32 [4, 64], replicated, may hold values from 0 to 63, as said below
- temporal_gain: bfloat16 [4, 512], P('section'), may hold values from 0.099609375 to 1.8984375
- temporal_qkv: bfloat16 [4, 512, 1536], P('section'), may hold values from -7 to 7
- temporal_out: bfloat16 [4, 512, 512], P('section'), may hold values from -0.25 to 0.25
- social_gain: bfloat16 [4, 512], P('section'), may hold values from 0.099609375 to 1.8984375
- social_qkv: bfloat16 [4, 512, 1536], P('section'), may hold values from -7 to 7
- social_out: bfloat16 [4, 512, 512], P('section'), may hold values from -0.25 to 0.25
Outputs:
- evolved: bfloat16 [4, 64, 128, 512], P('section', 'tok')
Inputs may be any that keep to these rules, and one draw needn't show every extreme that they name: `valid_steps`: each pedestrian's observed steps lie within one run of consecutive steps; any steps of that run, at its ends too and several in a row, may be unobserved. `hilbert_order`: each row names every pedestrian of the micro-batch once.
All inputs are finite; a program needn't handle non-finite values.
Results may differ from a plain program's by a relative error of at most 0.029.
Values may be sent and summed in bfloat16 or wider, within the bound.
A program may use at most 128 MiB of HBM per device.

v0:
```python
import functools

import jax
import jax.numpy as jnp
from jax import lax
from jax.experimental import pallas as pl
from jax.experimental.pallas import tpu as pltpu
from jax.sharding import PartitionSpec as P

H = 8
TW = 32
SW = 128
NEG_BIG = -1e30
EPSILON = 1e-05
MESH = pl.DeviceIdType.MESH
BF = jnp.bfloat16
F32 = jnp.float32


def sub_layer(src, gain, weight_qkv, weight_out, bias, stage):
    blocks, per_block, width = src.shape
    count = blocks * per_block
    head = width // H
    pair = 2 * head
    wide = src[...].reshape(count, width).astype(F32)
    inverse_rms = lax.rsqrt(jnp.mean(wide * wide, axis=-1, keepdims=True) + EPSILON)
    normed = (wide * inverse_rms * gain[...].astype(F32)).astype(BF)
    low = lax.broadcasted_iota(jnp.int32, (count, pair), 1) < head
    zero = jnp.zeros((count, pair), BF)
    bias_rows = bias[...]
    mixed = []
    group = 2 * pair
    for start in range(0, width, group):
        three = [
            jnp.dot(normed, weight_qkv[:, part * width + start : part * width + start + group],
                    preferred_element_type=F32)
            for part in range(3)
        ]
        query = (three[0] * head ** (-0.5)).astype(BF)
        key, value = three[1].astype(BF), three[2].astype(BF)
        for inner in range(0, group, pair):
            q = query[:, inner : inner + pair]
            k = key[:, inner : inner + pair]
            v = value[:, inner : inner + pair]
            both = jnp.concatenate([jnp.where(low, q, zero), jnp.where(low, zero, q)], axis=0)
            scores = lax.dot_general(both, k, (((1,), (1,)), ((), ())), preferred_element_type=F32)
            weights, sums = [], []
            for half in range(2):
                masked = scores[half * count : (half + 1) * count] + bias_rows
                expon = jnp.exp(masked - jnp.max(masked, axis=-1, keepdims=True))
                sums.append(jnp.sum(expon, axis=-1, keepdims=True))
                weights.append(expon.astype(BF))
            values = jnp.concatenate([jnp.where(low, v, zero), jnp.where(low, zero, v)], axis=0)
            blended = jnp.dot(jnp.concatenate(weights, axis=1), values, preferred_element_type=F32)
            scale = jnp.where(low, 1.0 / sums[0], 1.0 / sums[1])
            mixed.append((blended * scale).astype(BF))
    update = jnp.dot(jnp.concatenate(mixed, axis=1), weight_out[...], preferred_element_type=F32)
    stage[...] = (wide + update).astype(BF).reshape(blocks, per_block, width)


def kernel(
    sections, ways,
    tracks, valid, order, time_gain, crowd_gain,
    time_qkv_hbm, time_out_hbm, crowd_qkv_hbm, crowd_out_hbm,
    result,
    time_qkv, time_out, crowd_qkv, crowd_out,
    first, time_in, time_stage, crowd_in, crowd_stage, last_in,
    flag_stage, flag_in, time_bias, crowd_bias,
    weight_sem, first_sem, time_recv, time_send, crowd_recv, crowd_send,
    last_recv, flag_recv, flag_send, ready,
):
    section = lax.axis_index("section")
    me = lax.axis_index("tok")
    batches = time_in.shape[0]
    steps, width = tracks.shape
    per = steps // ways
    rows = steps

    loads = [
        pltpu.make_async_copy(hbm.at[0], held, weight_sem.at[i])
        for i, (hbm, held) in enumerate(
            ((time_qkv_hbm, time_qkv), (time_out_hbm, time_out),
             (crowd_qkv_hbm, crowd_qkv), (crowd_out_hbm, crowd_out))
        )
    ]
    for load in loads:
        load.start()

    barrier = pltpu.get_barrier_semaphore()

    @pl.when(section == 0)
    def _():
        for other in range(1, sections):
            pl.semaphore_signal(barrier, inc=1, device_id=(other, me), device_id_type=MESH)

        @pl.loop(1, ways)
        def _(step):
            pl.semaphore_signal(
                barrier, inc=1, device_id=(0, (me + step) % ways), device_id_type=MESH
            )

    @pl.when(section != 0)
    def _():
        pl.semaphore_signal(barrier, inc=1, device_id=(0, me), device_id_type=MESH)

    @pl.when(section == 0)
    def _():
        time_in[0] = tracks[...].reshape(ways, per, width)

    @pl.when(section != 0)
    def _():
        first[...] = tracks[...].reshape(ways, per, width)

    def first_copy(batch):
        return pltpu.make_async_remote_copy(
            src_ref=first, dst_ref=time_in.at[batch], send_sem=first_sem,
            recv_sem=time_recv.at[batch], device_id=(0, me), device_id_type=MESH,
        )

    @pl.when(section != 0)
    def _():
        pl.semaphore_wait(barrier, 1)
        first_copy(section).start()

    later = lax.broadcasted_iota(jnp.int32, (rows, rows), 0)
    earlier = lax.broadcasted_iota(jnp.int32, (rows, rows), 1)
    offset = later - earlier
    for batch in range(batches):
        flags = valid[batch]
        allowed = (offset >= 0) & (offset < TW) & ((flags == 1) | (offset == 0))
        time_bias[batch] = jnp.where(allowed, 0.0, NEG_BIG)
        flag_stage[batch : batch + 1, :] = flags.astype(F32).astype(BF)

    loads[0].wait()
    loads[1].wait()

    def exchange(src, dst, send_sem, recv_sem, target):
        @pl.when(target == section)
        def _():
            pltpu.make_async_copy(src.at[me], dst.at[me], recv_sem).start()

        @pl.when(target != section)
        def _():
            pltpu.make_async_remote_copy(
                src_ref=src.at[me], dst_ref=dst.at[me], send_sem=send_sem,
                recv_sem=recv_sem, device_id=(target, me), device_id_type=MESH,
            ).start()

        @pl.loop(1, ways)
        def _(step):
            peer = (me + step) % ways
            pltpu.make_async_remote_copy(
                src_ref=src.at[peer], dst_ref=dst.at[me], send_sem=send_sem,
                recv_sem=recv_sem, device_id=(target, peer), device_id_type=MESH,
            ).start()

    def exchange_flags():
        pltpu.make_async_copy(flag_stage, flag_in.at[me], flag_recv).start()

        @pl.loop(1, ways)
        def _(step):
            pltpu.make_async_remote_copy(
                src_ref=flag_stage, dst_ref=flag_in.at[me], send_sem=flag_send,
                recv_sem=flag_recv, device_id=(section, (me + step) % ways),
                device_id_type=MESH,
            ).start()

    def arrived(dst, recv_sem):
        pltpu.make_async_copy(dst, dst, recv_sem).wait()

    def sent(src, send_sem, local):
        @pl.when(local)
        def _():
            part = src.at[pl.ds(0, ways - 1)]
            pltpu.make_async_copy(part, part, send_sem).wait()

        @pl.when(jnp.logical_not(local))
        def _():
            pltpu.make_async_copy(src, src, send_sem).wait()

    @pl.loop(0, batches)
    def _(batch):
        @pl.when((section != 0) | (batch != 0))
        def _():
            arrived(time_in.at[batch], time_recv.at[batch])

        sub_layer(time_in.at[batch], time_gain, time_qkv, time_out,
                  time_bias.at[batch], time_stage.at[batch])

        @pl.when((section == 0) & (batch == 0))
        def _():
            pl.semaphore_wait(barrier, ways - 1 + sections - 1)

        @pl.when((section != 0) & (batch == 0))
        def _():
            pl.semaphore_wait(ready, 1)

        exchange(time_stage.at[batch], crowd_in.at[batch], time_send.at[batch],
                 crowd_recv.at[batch], section)

        @pl.when(batch == 0)
        def _():
            @pl.when(section == 0)
            def _():
                @pl.loop(1, ways)
                def _(step):
                    pl.semaphore_signal(
                        ready, inc=1, device_id=(0, (me + step) % ways), device_id_type=MESH
                    )

            exchange_flags()

    loads[2].wait()
    loads[3].wait()

    @pl.when(section == 0)
    def _():
        pl.semaphore_wait(ready, ways - 1)
        for other in range(1, sections):
            pl.semaphore_signal(ready, inc=1, device_id=(other, me), device_id_type=MESH)

    arrived(flag_in, flag_recv)
    row_of = lax.broadcasted_iota(jnp.int32, (rows, rows), 0)
    col_of = lax.broadcasted_iota(jnp.int32, (rows, rows), 1)
    pick = (row_of == me * per + col_of % per).astype(F32).astype(BF)
    every = jnp.dot(flag_in[...].reshape(ways * batches, steps), pick, preferred_element_type=F32)
    pair_row = lax.broadcasted_iota(jnp.int32, (ways * batches, rows), 0)
    pair_col = lax.broadcasted_iota(jnp.int32, (ways * batches, rows), 1)
    agents = order.shape[1]
    who = lax.broadcasted_iota(jnp.int32, (rows, agents), 0) // per
    place = lax.broadcasted_iota(jnp.int32, (rows, agents), 1)
    same_step = row_of % per == col_of % per
    itself = row_of == col_of
    for batch in range(batches):
        own = pair_row == (pair_col // per) * batches + batch
        flags = jnp.sum(jnp.where(own, every, 0.0), axis=0, keepdims=True)
        curve_col = jnp.sum(
            jnp.where(order[batch : batch + 1, :] == who, place, 0), axis=1, keepdims=True
        )
        curve_row = jnp.sum(jnp.where(itself, curve_col, 0), axis=0, keepdims=True)
        in_band = jnp.abs(curve_col - curve_row) <= SW
        allowed = same_step & in_band & ((flags == 1.0) | itself)
        crowd_bias[batch] = jnp.where(allowed, 0.0, NEG_BIG)

    @pl.loop(0, batches)
    def _(batch):
        arrived(crowd_in.at[batch], crowd_recv.at[batch])
        sub_layer(crowd_in.at[batch], crowd_gain, crowd_qkv, crowd_out,
                  crowd_bias.at[batch], crowd_stage.at[batch])

        @pl.when(section < sections - 1)
        def _():
            exchange(crowd_stage.at[batch], time_in.at[batch], crowd_send.at[batch],
                     time_recv.at[batch], section + 1)

        @pl.when(section == sections - 1)
        def _():
            exchange(crowd_stage.at[batch], last_in, crowd_send.at[batch], last_recv, batch)

    arrived(last_in, last_recv)
    result[...] = last_in[...].reshape(steps, width)

    @pl.when(section != 0)
    def _():
        first_copy(section).wait_send()

    part = flag_in.at[pl.ds(0, ways - 1)]
    pltpu.make_async_copy(part, part, flag_send).wait()

    @pl.loop(0, batches)
    def _(batch):
        part = time_stage.at[batch, pl.ds(0, ways - 1)]
        pltpu.make_async_copy(part, part, time_send.at[batch]).wait()
        sent(crowd_stage.at[batch], crowd_send.at[batch],
             (section == sections - 1) & (batch == sections - 1))


def body(
    tracks, valid_steps, hilbert_order,
    temporal_gain, temporal_qkv, temporal_out,
    social_gain, social_qkv, social_out,
):
    sections, ways = lax.axis_size("section"), lax.axis_size("tok")
    _, _, steps, width = tracks.shape
    batches = valid_steps.shape[0]
    per = steps // ways
    block = (ways, per, width)
    vmem = pl.BlockSpec(memory_space=pltpu.VMEM)
    hbm = pl.BlockSpec(memory_space=pltpu.HBM)
    dma = pltpu.SemaphoreType.DMA
    out = pl.pallas_call(
        functools.partial(kernel, sections, ways),
        out_shape=jax.ShapeDtypeStruct((steps, width), BF),
        in_specs=[vmem] * 5 + [hbm] * 4,
        out_specs=vmem,
        scratch_shapes=[
            pltpu.VMEM(temporal_qkv.shape[1:], BF),
            pltpu.VMEM(temporal_out.shape[1:], BF),
            pltpu.VMEM(social_qkv.shape[1:], BF),
            pltpu.VMEM(social_out.shape[1:], BF),
            pltpu.VMEM(block, BF),
            pltpu.VMEM((batches,) + block, BF),
            pltpu.VMEM((batches,) + block, BF),
            pltpu.VMEM((batches,) + block, BF),
            pltpu.VMEM((batches,) + block, BF),
            pltpu.VMEM(block, BF),
            pltpu.VMEM((batches, steps), BF),
            pltpu.VMEM((ways, batches, steps), BF),
            pltpu.VMEM((batches, steps, steps), F32),
            pltpu.VMEM((batches, steps, steps), F32),
            dma((4,)), dma, dma((batches,)), dma((batches,)), dma((batches,)), dma((batches,)),
            dma, dma, dma, pltpu.SemaphoreType.REGULAR,
        ],
        compiler_params=pltpu.CompilerParams(
            collective_id=0, has_side_effects=True, vmem_limit_bytes=48 * 1024 * 1024
        ),
        name="layers",
    )(
        tracks.reshape(steps, width), valid_steps, hilbert_order, temporal_gain, social_gain,
        temporal_qkv, temporal_out, social_qkv, social_out,
    )
    return out.reshape(tracks.shape)


def solution(mesh):
    placed = (
        P("section", "tok", None, None),
        P(None, "tok", None),
        P(),
        P("section", None),
        P("section", None, None),
        P("section", None, None),
        P("section", None),
        P("section", None, None),
        P("section", None, None),
    )
    return jax.shard_map(
        body, mesh=mesh, in_specs=placed, out_specs=P("section", "tok", None, None), check_vma=False
    )
```

profile of v0, /device:TPU:7, one launch (start us, length us, event | category | flops | bytes accessed | tf_op | source)
XLA Modules:
  0.0 113.3 jit_solution(17528590512808298201)
XLA Ops:
  0.0 0.0 copy-start
  0.0 1.4 %copy-done = bf16[1,512,1536]{2,1,0:T(8,128)(2,1)S(1)} copy-done((bf16[1,512,1536]{2,1,0:T(8,128)(2,1)S(1)}, bf16[1,512,1536]{2,1,0:T(8,128)(2,1)}, u32[]{:S(2)}) %copy-start) | copy-done | bytes 1572888
  1.4 0.0 copy-start.1
  1.4 1.4 %copy-done.1 = bf16[1,512,1536]{2,1,0:T(8,128)(2,1)S(1)} copy-done((bf16[1,512,1536]{2,1,0:T(8,128)(2,1)S(1)}, bf16[1,512,1536]{2,1,0:T(8,128)(2,1)}, u32[]{:S(2)}) %copy-start.1) | copy-done | bytes 1572888
  2.8 0.0 copy-start.2
  2.8 1.0 copy-done.2
  3.9 0.0 copy-start.3
  3.9 1.0 copy-done.3
  4.9 0.0 copy-start.4
  4.9 0.9 copy-done.4
  5.8 0.0 copy-start.5
  5.8 0.7 copy-done.5
  6.5 0.0 copy-start.6
  6.5 0.7 copy-done.6
  7.2 0.0 copy-start.7
  7.2 0.7 copy-done.7
  7.9 0.0 copy-start.8
  7.9 0.7 copy-done.8
  8.5 104.1 %layers.1 = bf16[128,512]{1,0:T(8,128)(2,1)S(1)} custom-call(bf16[128,512]{1,0:T(8,128)(2,1)S(1)} %bitcast.3, s32[4,1,128]{2,1,0:T(1,128)S(1)} %copy-done.5, s32[4,64]{1,0:T(4,128)S(1)} %copy-done.6, bf16[1,512]{1,0:T(2,128)(2,1)S(1)} %copy-done.7, bf16[1,512]{1,0:T(2,128)(2,1)S(1)} %copy-done.8, bf16[1,512,1536]{2,1,0:T(8,128)(2,1)S(1)} %copy-done, ...), custom_call_target="tpu_custom_call" | custom-call | tf_op jit(solution)/shard_map/layers/pallas_call | solution.py:291
  112.6 0.7 copy.11
Async XLA Ops:
  0.0 1.4 %copy-start = (bf16[1,512,1536]{2,1,0:T(8,128)(2,1)S(1)}, bf16[1,512,1536]{2,1,0:T(8,128)(2,1)}, u32[]{:S(2)}) copy-start(bf16[1,512,1536]{2,1,0:T(8,128)(2,1)} %time_qkv_hbm.1) | copy-start | bytes 4718596
  1.4 1.4 %copy-start.1 = (bf16[1,512,1536]{2,1,0:T(8,128)(2,1)S(1)}, bf16[1,512,1536]{2,1,0:T(8,128)(2,1)}, u32[]{:S(2)}) copy-start(bf16[1,512,1536]{2,1,0:T(8,128)(2,1)} %crowd_qkv_hbm.1) | copy-start | bytes 4718596
  2.8 1.0 copy-start.2
  3.9 1.0 copy-start.3
  4.9 0.9 copy-start.4
  5.8 0.7 copy-start.5
  6.5 0.7 copy-start.6
  7.2 0.7 copy-start.7
  7.9 0.7 copy-start.8
where the time goes:
time: 114 us; the launch traced here: 113 us
  Pallas kernels  104 us (91%)
  local copies, waits for them, and re-layouts  9.18 us (8%)
    pallas_call x1, Pallas kernels, body(): pl.pallas_call(functools.partial(kernel, sections, ways), out_shape=jax.S...  104 us
    unnamed x19, local copies, waits for them, and re-layouts  9.18 us

commit v1 on v0

--- a/solution.py
+++ b/solution.py
@@ -60,13 +60,14 @@
 
 def kernel(
     sections, ways,
-    tracks, valid, order, time_gain, crowd_gain,
+    tracks_hbm, valid_hbm, order_hbm, time_gain_hbm, crowd_gain_hbm,
     time_qkv_hbm, time_out_hbm, crowd_qkv_hbm, crowd_out_hbm,
     result,
+    tracks, valid, order, time_gain, crowd_gain,
     time_qkv, time_out, crowd_qkv, crowd_out,
     first, time_in, time_stage, crowd_in, crowd_stage, last_in,
     flag_stage, flag_in, time_bias, crowd_bias,
-    weight_sem, first_sem, time_recv, time_send, crowd_recv, crowd_send,
+    load_sem, first_sem, time_recv, time_send, crowd_recv, crowd_send,
     last_recv, flag_recv, flag_send, ready,
 ):
     section = lax.axis_index("section")
@@ -77,14 +78,17 @@
     rows = steps
 
     loads = [
-        pltpu.make_async_copy(hbm.at[0], held, weight_sem.at[i])
-        for i, (hbm, held) in enumerate(
-            ((time_qkv_hbm, time_qkv), (time_out_hbm, time_out),
-             (crowd_qkv_hbm, crowd_qkv), (crowd_out_hbm, crowd_out))
-        )
+        pltpu.make_async_copy(hbm, held, load_sem.at[i])
+        for i, (hbm, held) in enumerate((
+            (tracks_hbm, tracks), (time_gain_hbm, time_gain), (valid_hbm, valid),
+            (time_qkv_hbm.at[0], time_qkv), (time_out_hbm.at[0], time_out),
+            (order_hbm, order), (crowd_gain_hbm, crowd_gain),
+            (crowd_qkv_hbm.at[0], crowd_qkv), (crowd_out_hbm.at[0], crowd_out),
+        ))
     ]
     for load in loads:
         load.start()
+    tracks_load, gain_load, valid_load, qkv_load, out_load = loads[:5]
 
     barrier = pltpu.get_barrier_semaphore()
 
@@ -103,6 +107,8 @@
     def _():
         pl.semaphore_signal(barrier, inc=1, device_id=(0, me), device_id_type=MESH)
 
+    tracks_load.wait()
+
     @pl.when(section == 0)
     def _():
         time_in[0] = tracks[...].reshape(ways, per, width)
@@ -125,14 +131,16 @@
     later = lax.broadcasted_iota(jnp.int32, (rows, rows), 0)
     earlier = lax.broadcasted_iota(jnp.int32, (rows, rows), 1)
     offset = later - earlier
+    valid_load.wait()
     for batch in range(batches):
         flags = valid[batch]
         allowed = (offset >= 0) & (offset < TW) & ((flags == 1) | (offset == 0))
         time_bias[batch] = jnp.where(allowed, 0.0, NEG_BIG)
         flag_stage[batch : batch + 1, :] = flags.astype(F32).astype(BF)
 
-    loads[0].wait()
-    loads[1].wait()
+    gain_load.wait()
+    qkv_load.wait()
+    out_load.wait()
 
     def exchange(src, dst, send_sem, recv_sem, target):
         @pl.when(target == section)
@@ -210,8 +218,8 @@
 
             exchange_flags()
 
-    loads[2].wait()
-    loads[3].wait()
+    for load in loads[5:]:
+        load.wait()
 
     @pl.when(section == 0)
     def _():
@@ -291,9 +299,14 @@
     out = pl.pallas_call(
         functools.partial(kernel, sections, ways),
         out_shape=jax.ShapeDtypeStruct((steps, width), BF),
-        in_specs=[vmem] * 5 + [hbm] * 4,
+        in_specs=[hbm] * 9,
         out_specs=vmem,
         scratch_shapes=[
+            pltpu.VMEM((steps, width), BF),
+            pltpu.VMEM(valid_steps.shape, valid_steps.dtype),
+            pltpu.VMEM(hilbert_order.shape, hilbert_order.dtype),
+            pltpu.VMEM(temporal_gain.shape, BF),
+            pltpu.VMEM(social_gain.shape, BF),
             pltpu.VMEM(temporal_qkv.shape[1:], BF),
             pltpu.VMEM(temporal_out.shape[1:], BF),
             pltpu.VMEM(social_qkv.shape[1:], BF),
@@ -308,11 +321,11 @@
             pltpu.VMEM((ways, batches, steps), BF),
             pltpu.VMEM((batches, steps, steps), F32),
             pltpu.VMEM((batches, steps, steps), F32),
-            dma((4,)), dma, dma((batches,)), dma((batches,)), dma((batches,)), dma((batches,)),
+            dma((9,)), dma, dma((batches,)), dma((batches,)), dma((batches,)), dma((batches,)),
             dma, dma, dma, pltpu.SemaphoreType.REGULAR,
         ],
         compiler_params=pltpu.CompilerParams(
-            collective_id=0, has_side_effects=True, vmem_limit_bytes=48 * 1024 * 1024
+            collective_id=0, has_side_effects=True, vmem_limit_bytes=67_043_328
         ),
         name="layers",
     )(

time: 114 us -> 107 us (0.939)
  local copies, waits for them, and re-layouts: 9.18 us -> 1.57 us
    unnamed x19 -> x1, local copies, waits for them, and re-layouts: 9.18 us -> 1.57 us
where the time goes in v1:
time: 107 us
  Pallas kernels  105 us (98%)
  local copies, waits for them, and re-layouts  1.57 us (1%)
    pallas_call x1, Pallas kernels, body(): pl.pallas_call(functools.partial(kernel, sections, ways), out_shape=jax.S...  105 us

profile of v1, /device:TPU:7, one launch (start us, length us, event | category | flops | bytes accessed | tf_op | source)
XLA Modules:
  0.0 106.6 jit_solution(12463912091820718634)
XLA Ops:
  0.0 105.1 %layers.1 = bf16[128,512]{1,0:T(8,128)(2,1)} custom-call(bf16[128,512]{1,0:T(8,128)(2,1)} %bitcast.3, s32[4,1,128]{2,1,0:T(1,128)} %valid_hbm.1, s32[4,64]{1,0:T(4,128)} %order_hbm.1, bf16[1,512]{1,0:T(2,128)(2,1)} %time_gain_hbm.1, bf16[1,512]{1,0:T(2,128)(2,1)} %crowd_gain_hbm.1, bf16[1,512,1536]{2,1,0:T(8,128)(2,1)} %time_qkv_hbm.1, ...), custom_call_target="tpu_custom_call" | custom-call | tf_op jit(solution)/shard_map/layers/pallas_call | solution.py:299
  105.1 1.6 %copy.11 = bf16[1,1,128,512]{3,2,1,0:T(8,128)(2,1)} copy(bf16[1,1,128,512]{3,2,1,0:T(8,128)(2,1)} %bitcast.2) | data formatting | bytes 262144

commit v2 on v1

--- a/solution.py
+++ b/solution.py
@@ -186,8 +186,7 @@
         def _():
             pltpu.make_async_copy(src, src, send_sem).wait()
 
-    @pl.loop(0, batches)
-    def _(batch):
+    def temporal(batch):
         @pl.when((section != 0) | (batch != 0))
         def _():
             arrived(time_in.at[batch], time_recv.at[batch])
@@ -198,60 +197,47 @@
         @pl.when((section == 0) & (batch == 0))
         def _():
             pl.semaphore_wait(barrier, ways - 1 + sections - 1)
-
-        @pl.when((section != 0) & (batch == 0))
-        def _():
-            pl.semaphore_wait(ready, 1)
+            exchange_flags()
 
         exchange(time_stage.at[batch], crowd_in.at[batch], time_send.at[batch],
                  crowd_recv.at[batch], section)
 
-        @pl.when(batch == 0)
-        def _():
-            @pl.when(section == 0)
-            def _():
-                @pl.loop(1, ways)
-                def _(step):
-                    pl.semaphore_signal(
-                        ready, inc=1, device_id=(0, (me + step) % ways), device_id_type=MESH
-                    )
-
-            exchange_flags()
-
-    for load in loads[5:]:
-        load.wait()
-
-    @pl.when(section == 0)
-    def _():
-        pl.semaphore_wait(ready, ways - 1)
-        for other in range(1, sections):
-            pl.semaphore_signal(ready, inc=1, device_id=(other, me), device_id_type=MESH)
-
-    arrived(flag_in, flag_recv)
-    row_of = lax.broadcasted_iota(jnp.int32, (rows, rows), 0)
-    col_of = lax.broadcasted_iota(jnp.int32, (rows, rows), 1)
-    pick = (row_of == me * per + col_of % per).astype(F32).astype(BF)
-    every = jnp.dot(flag_in[...].reshape(ways * batches, steps), pick, preferred_element_type=F32)
-    pair_row = lax.broadcasted_iota(jnp.int32, (ways * batches, rows), 0)
-    pair_col = lax.broadcasted_iota(jnp.int32, (ways * batches, rows), 1)
-    agents = order.shape[1]
-    who = lax.broadcasted_iota(jnp.int32, (rows, agents), 0) // per
-    place = lax.broadcasted_iota(jnp.int32, (rows, agents), 1)
-    same_step = row_of % per == col_of % per
-    itself = row_of == col_of
-    for batch in range(batches):
-        own = pair_row == (pair_col // per) * batches + batch
-        flags = jnp.sum(jnp.where(own, every, 0.0), axis=0, keepdims=True)
-        curve_col = jnp.sum(
-            jnp.where(order[batch : batch + 1, :] == who, place, 0), axis=1, keepdims=True
-        )
-        curve_row = jnp.sum(jnp.where(itself, curve_col, 0), axis=0, keepdims=True)
-        in_band = jnp.abs(curve_col - curve_row) <= SW
-        allowed = same_step & in_band & ((flags == 1.0) | itself)
-        crowd_bias[batch] = jnp.where(allowed, 0.0, NEG_BIG)
-
-    @pl.loop(0, batches)
-    def _(batch):
+        @pl.when((section == 0) & (batch == 0))
+        def _():
+            @pl.loop(1, ways)
+            def _(step):
+                pl.semaphore_signal(
+                    ready, inc=1, device_id=(0, (me + step) % ways), device_id_type=MESH
+                )
+
+    def crowd_masks():
+        for load in loads[5:]:
+            load.wait()
+
+        arrived(flag_in, flag_recv)
+        row_of = lax.broadcasted_iota(jnp.int32, (rows, rows), 0)
+        col_of = lax.broadcasted_iota(jnp.int32, (rows, rows), 1)
+        pick = (row_of == me * per + col_of % per).astype(F32).astype(BF)
+        every = jnp.dot(flag_in[...].reshape(ways * batches, steps), pick, preferred_element_type=F32)
+        pair_row = lax.broadcasted_iota(jnp.int32, (ways * batches, rows), 0)
+        pair_col = lax.broadcasted_iota(jnp.int32, (ways * batches, rows), 1)
+        agents = order.shape[1]
+        who = lax.broadcasted_iota(jnp.int32, (rows, agents), 0) // per
+        place = lax.broadcasted_iota(jnp.int32, (rows, agents), 1)
+        same_step = row_of % per == col_of % per
+        itself = row_of == col_of
+        for batch in range(batches):
+            own = pair_row == (pair_col // per) * batches + batch
+            flags = jnp.sum(jnp.where(own, every, 0.0), axis=0, keepdims=True)
+            curve_col = jnp.sum(
+                jnp.where(order[batch : batch + 1, :] == who, place, 0), axis=1, keepdims=True
+            )
+            curve_row = jnp.sum(jnp.where(itself, curve_col, 0), axis=0, keepdims=True)
+            in_band = jnp.abs(curve_col - curve_row) <= SW
+            allowed = same_step & in_band & ((flags == 1.0) | itself)
+            crowd_bias[batch] = jnp.where(allowed, 0.0, NEG_BIG)
+
+    def social(batch):
         arrived(crowd_in.at[batch], crowd_recv.at[batch])
         sub_layer(crowd_in.at[batch], crowd_gain, crowd_qkv, crowd_out,
                   crowd_bias.at[batch], crowd_stage.at[batch])
@@ -264,6 +250,31 @@
         @pl.when(section == sections - 1)
         def _():
             exchange(crowd_stage.at[batch], last_in, crowd_send.at[batch], last_recv, batch)
+
+    @pl.when(section != 0)
+    def _():
+        pl.semaphore_wait(ready, 1)
+        exchange_flags()
+
+    @pl.loop(0, batches + 1)
+    def _(turn):
+        @pl.when(turn < batches)
+        def _():
+            temporal(turn)
+
+        @pl.when((section == 0) & (turn == 1))
+        def _():
+            pl.semaphore_wait(ready, ways - 1)
+            for other in range(1, sections):
+                pl.semaphore_signal(ready, inc=1, device_id=(other, me), device_id_type=MESH)
+
+        @pl.when(((section == 0) & (turn == 1)) | ((section != 0) & (turn == 0)))
+        def _():
+            crowd_masks()
+
+        @pl.when(turn > 0)
+        def _():
+            social(turn - 1)
 
     arrived(last_in, last_recv)
     result[...] = last_in[...].reshape(steps, width)

time: 107 us -> 101 us (0.944)
  Pallas kernels: 105 us -> 98.9 us
    pallas_call x1, Pallas kernels: 105 us -> 98.9 us  [body(): pl.pallas_call(functools.partial(kernel, sections, ways), out_shape=jax.S...]
where the time goes in v2:
time: 101 us; the launch traced here: 100 us
  Pallas kernels  98.9 us (98%)
  local copies, waits for them, and re-layouts  1.57 us (2%)
    pallas_call x1, Pallas kernels, body(): pl.pallas_call(functools.partial(kernel, sections, ways), out_shape=jax.S...  98.9 us

profile of v2, /device:TPU:7, one launch (start us, length us, event | category | flops | bytes accessed | tf_op | source)
XLA Modules:
  0.0 100.5 jit_solution(14643554355005519738)
XLA Ops:
  0.0 98.9 %layers.1 = bf16[128,512]{1,0:T(8,128)(2,1)} custom-call(bf16[128,512]{1,0:T(8,128)(2,1)} %bitcast.3, s32[4,1,128]{2,1,0:T(1,128)} %valid_hbm.1, s32[4,64]{1,0:T(4,128)} %order_hbm.1, bf16[1,512]{1,0:T(2,128)(2,1)} %time_gain_hbm.1, bf16[1,512]{1,0:T(2,128)(2,1)} %crowd_gain_hbm.1, bf16[1,512,1536]{2,1,0:T(8,128)(2,1)} %time_qkv_hbm.1, ...), custom_call_target="tpu_custom_call" | custom-call | tf_op jit(solution)/shard_map/layers/pallas_call | solution.py:310
  98.9 1.6 %copy.11 = bf16[1,1,128,512]{3,2,1,0:T(8,128)(2,1)} copy(bf16[1,1,128,512]{3,2,1,0:T(8,128)(2,1)} %bitcast.2) | data formatting | bytes 262144

commit v3 on v2

--- a/solution.py
+++ b/solution.py
@@ -154,7 +154,7 @@
                 recv_sem=recv_sem, device_id=(target, me), device_id_type=MESH,
             ).start()
 
-        @pl.loop(1, ways)
+        @pl.loop(1, ways, unroll=3)
         def _(step):
             peer = (me + step) % ways
             pltpu.make_async_remote_copy(

time: 101 us -> 103 us (1.020)
  Pallas kernels: 98.9 us -> 101 us
    pallas_call x1, Pallas kernels: 98.9 us -> 101 us  [body(): pl.pallas_call(functools.partial(kernel, sections, ways), out_shape=jax.S...]
where the time goes in v3:
time: 103 us; the launch traced here: 102 us
  Pallas kernels  101 us (98%)
  local copies, waits for them, and re-layouts  1.57 us (2%)
    pallas_call x1, Pallas kernels, body(): pl.pallas_call(functools.partial(kernel, sections, ways), out_shape=jax.S...  101 us

profile of v3, /device:TPU:7, one launch (start us, length us, event | category | flops | bytes accessed | tf_op | source)
XLA Modules:
  0.0 102.5 jit_solution(11188053890394952447)
XLA Ops:
  0.0 100.9 %layers.1 = bf16[128,512]{1,0:T(8,128)(2,1)} custom-call(bf16[128,512]{1,0:T(8,128)(2,1)} %bitcast.3, s32[4,1,128]{2,1,0:T(1,128)} %valid_hbm.1, s32[4,64]{1,0:T(4,128)} %order_hbm.1, bf16[1,512]{1,0:T(2,128)(2,1)} %time_gain_hbm.1, bf16[1,512]{1,0:T(2,128)(2,1)} %crowd_gain_hbm.1, bf16[1,512,1536]{2,1,0:T(8,128)(2,1)} %time_qkv_hbm.1, ...), custom_call_target="tpu_custom_call" | custom-call | tf_op jit(solution)/shard_map/layers/pallas_call | solution.py:310
  100.9 1.6 %copy.11 = bf16[1,1,128,512]{3,2,1,0:T(8,128)(2,1)} copy(bf16[1,1,128,512]{3,2,1,0:T(8,128)(2,1)} %bitcast.2) | data formatting | bytes 262144
